TPU v7x, 32 devices: a whole 2x2x4 slice. The times are simulated.
32 devices in a mesh: row: 4 (over y, x), col: 8 (over z, core).
Axes of the slice: x: 2, y: 2, z: 4, core: 2. Of those that a mesh axis runs over, the one named last changes fastest.
Arguments:
- noise_points: float32 [16384, 512], P('row'), may hold values from -30 to 30
- data_points: float32 [2048, 512], P('col'), may hold values from -30 to 30
- times: float32 [16384, 8], P(('row', 'col')), may hold values from 0 to 1
- time_shift: float32 [1024], replicated, may hold values from -6 to 6
- weight_in: bfloat16 [512, 1024], replicated, may hold values from -0.25 to 0.25
- weight_out: bfloat16 [1024, 512], replicated, may hold values from -0.1875 to 0.1875
Outputs:
- predicted: bfloat16 [131072, 512], P(('row', 'col'))
- grad_in: float32 [512, 1024], replicated
- grad_out: float32 [1024, 512], replicated
All inputs are finite; a program needn't handle non-finite values.
Results may differ from a plain program's by a relative error of at most 0.0057.
Values sent between devices are 32-bit elements; how exact they have to be, the bound alone decides.
No kernel may reach another device: no remote copies, remote signals or barrier semaphores. Data moves between devices by JAX's collectives and lax.ppermute only.
A program may use at most 128 MiB of HBM per device.

v0:
```python
import math
import jax
import jax.numpy as jnp
from jax import lax
from jax.sharding import PartitionSpec as P

ENTROPY = 0.05
HIGHEST_PREC = lax.Precision.HIGHEST


def combined_all(part, axis, combine):
    gathered = jax.tree.map(lambda a: lax.all_gather(a, axis), part)

    def take(source):
        return jax.tree.map(lambda a: lax.dynamic_index_in_dim(a, source, 0, False), gathered)

    return lax.fori_loop(
        1, lax.axis_size(axis), lambda source, state: combine(state, take(source)), take(0)
    )


def combine_pairs(first, second):
    new_peak = jnp.maximum(first[0], second[0])
    total = first[1] * jnp.exp(first[0] - new_peak) + second[1] * jnp.exp(second[0] - new_peak)
    return (new_peak, total)


def on_device(noise_points, data_points, times, time_shift, weight_in, weight_out):
    count_row = lax.axis_size("row")
    count_col = lax.axis_size("col")
    rows_here = noise_points.shape[0]
    cols_here = data_points.shape[0]
    total_noise = rows_here * count_row
    total_data = cols_here * count_col
    width = noise_points.shape[1]
    noise_sq = jnp.sum(noise_points * noise_points, axis=1)
    data_sq = jnp.sum(data_points * data_points, axis=1)
    inner = jnp.dot(
        noise_points, data_points.T, precision=HIGHEST_PREC, preferred_element_type=jnp.float32
    )
    cost = (noise_sq[:, None] + data_sq[None, :] - 2.0 * inner) / width
    potential_g = jnp.zeros((cols_here,), jnp.float32)
    scores = (potential_g[None, :] - cost) / ENTROPY
    local_peak = jnp.max(scores, axis=1)
    local_total = jnp.sum(jnp.exp(scores - local_peak[:, None]), axis=1)
    row_peak, row_total = combined_all((local_peak, local_total), "col", combine_pairs)
    potential_f = -ENTROPY * (row_peak + jnp.log(row_total) - math.log(float(total_data)))
    scores = (potential_f[:, None] - cost) / ENTROPY
    local_peak = jnp.max(scores, axis=0)
    local_total = jnp.sum(jnp.exp(scores - local_peak[None, :]), axis=0)
    col_peak, col_total = combined_all((local_peak, local_total), "row", combine_pairs)
    potential_g = -ENTROPY * (col_peak + jnp.log(col_total) - math.log(float(total_noise)))
    scores = (potential_g[None, :] - cost) / ENTROPY
    final_peak = lax.pmax(jnp.max(scores, axis=1), "col")
    weights = jnp.exp(scores - final_peak[:, None])
    numer = jnp.dot(
        weights, data_points, precision=HIGHEST_PREC, preferred_element_type=jnp.float32
    )
    denom = jnp.sum(weights, axis=1)
    numer_rows, denom_rows = (
        lax.psum_scatter(numer, "col", scatter_dimension=0, tiled=True),
        lax.psum_scatter(denom, "col", scatter_dimension=0, tiled=True),
    )
    target = numer_rows / denom_rows[:, None]
    share = rows_here // count_col
    anchor = lax.dynamic_slice_in_dim(noise_points, lax.axis_index("col") * share, share, 0)
    steps_each = times.shape[1]
    tvals = times[:, :, None]
    mixed = (
        ((1.0 - tvals) * anchor[:, None, :] + tvals * target[:, None, :])
        .reshape(share * steps_each, width)
        .astype(jnp.bfloat16)
    )
    velocity = jnp.broadcast_to((target - anchor)[:, None, :], (share, steps_each, width)).reshape(
        share * steps_each, width
    )
    hid_width = weight_in.shape[1]
    pre = (
        jnp.dot(mixed, weight_in, preferred_element_type=jnp.float32)
        + times.reshape(share * steps_each, 1) * time_shift[None, :]
    )
    hidden = jax.nn.silu(pre).astype(jnp.bfloat16)
    output = jnp.dot(hidden, weight_out, preferred_element_type=jnp.float32)
    predicted = output.astype(jnp.bfloat16)
    scale = 1.0 / math.sqrt(float(total_noise * steps_each))
    delta = ((output - velocity) * scale).astype(jnp.bfloat16)
    back = lax.dot_general(
        delta, weight_out, (((1,), (1,)), ((), ())), preferred_element_type=jnp.float32
    )
    sig = jax.nn.sigmoid(pre)
    delta_pre = (back * sig * (1.0 + pre * (1.0 - sig))).astype(jnp.bfloat16)
    contract = (((0,), (0,)), ((), ()))
    first = lax.dot_general(mixed, delta_pre, contract, preferred_element_type=jnp.float32)
    second = lax.dot_general(delta, hidden, contract, preferred_element_type=jnp.float32)
    summed = lax.psum(jnp.concatenate([first, second], axis=1), ("row", "col"))
    grad_in = summed[:, :hid_width]
    grad_out = summed[:, hid_width:].T
    return (predicted, grad_in, grad_out)


def solution(mesh):
    in_specs = (P("row", None), P("col", None), P(("row", "col"), None), P(), P(), P())
    out_specs = (P(("row", "col"), None), P(), P())
    return jax.shard_map(
        on_device, mesh=mesh, in_specs=in_specs, out_specs=out_specs, check_vma=False
    )
```

profile of v0, /device:TPU:0, one launch (start us, length us, event | category | flops | bytes accessed | tf_op | source)
XLA Modules:
  0.0 410.7 jit_solution(17883860172667304204)
XLA Ops:
  7.2 0.0 copy-start
  7.2 0.0 reduce-scatter.2.cloned.1.call-start
  7.2 1.3 multiply_reduce_fusion.1
  8.5 4.2 %multiply_reduce_fusion = f32[4096]{0:T(1024)S(1)} fusion(f32[4096,512]{1,0:T(8,128)} %param.10), kind=kLoop, calls=%fused_computation.17 | loop fusion | flops 4190208 | bytes 8404992 | tf_op jit(solution)/shard_map/reduce_sum | solution.py:36
  12.7 1.6 copy-done.3
  14.3 9.3 %fusion.20 = (f32[4096]{0:T(1024)S(1)}, f32[4096,256]{0,1:T(8,128)}) fusion(f32[4096,512]{1,0:T(8,128)S(1)} %copy-done.3, f32[256,512]{1,0:T(8,128)S(1)} %copy-done.4, f32[256]{0:T(256)S(1)} %multiply_reduce_fusion.1, f32[4096]{0:T(1024)S(1)} %multiply_reduce_fusion), kind=kOutput, calls=%fused_computation.39 | convolution fusion | flops 6449786880 | bytes 13140992 | tf_op jit(solution)/shard_map/dot_general | solution.py:38
  23.6 15.7 %all-gather = f32[32768]{0:T(1024)S(1)} all-gather(f32[4096]{0:T(1024)S(1)} %get-tuple-element.315), channel_id=2, replica_groups=mesh['row'=4,'col'=8] {'col'}, dimensions={0}, use_global_device_ids=true | all-gather | bytes 147456 | tf_op jit(solution)/shard_map/all_gather | solution.py:12
  39.3 3.0 exponential_reduce_fusion.1
  42.4 14.0 %all-gather.1 = f32[32768]{0:T(1024)S(1)} all-gather(f32[4096]{0:T(1024)S(1)} %exponential_reduce_fusion.1), channel_id=3, replica_groups=mesh['row'=4,'col'=8] {'col'}, dimensions={0}, use_global_device_ids=true | all-gather | bytes 147456 | tf_op jit(solution)/shard_map/all_gather | solution.py:12
  56.4 0.6 while.34
  57.0 0.0 copy-start.2
  57.0 2.9 fusion.21
  59.9 0.6 copy-done.2
  60.4 0.9 exponential_reduce_fusion
  61.4 8.1 %all-gather.4 = f32[4,1,256]{2,1,0:T(1,128)S(1)} all-gather(f32[1,1,256]{2,1,0:T(1,128)S(1)} %bitcast.83), channel_id=4, replica_groups=mesh['row'=4,'col'=8] {'row'}, dimensions={0}, use_global_device_ids=true | all-gather | bytes 5120 | tf_op jit(solution)/shard_map/all_gather | solution.py:12
  69.5 8.0 %all-gather.5 = f32[4,1,256]{2,1,0:T(1,128)S(1)} all-gather(f32[1,1,256]{2,1,0:T(1,128)S(1)} %bitcast.84), channel_id=5, replica_groups=mesh['row'=4,'col'=8] {'row'}, dimensions={0}, use_global_device_ids=true | all-gather | bytes 5120 | tf_op jit(solution)/shard_map/all_gather | solution.py:12
  77.5 0.1 while.35
  77.7 2.8 fusion.22
  80.4 26.1 %pmax.7 = f32[4096]{0:T(1024)S(1)} all-reduce(f32[4096]{0:T(1024)S(1)} %fusion.22), channel_id=1, replica_groups=mesh['row'=4,'col'=8] {'col'}, use_global_device_ids=true, to_apply=%region_11.12 | all-reduce | flops 4096 | bytes 32768 | tf_op jit(solution)/shard_map/pmax | solution.py:54
  106.5 11.1 %fusion.24 = f32[4096,512]{1,0:T(8,128)} fusion(f32[256,512]{1,0:T(8,128)S(1)} %copy-done.4, f32[4096,256]{0,1:T(8,128)} %get-tuple-element.316, f32[4096]{0:T(1024)S(1)} %pmax.7, f32[256]{0:T(256)S(1)} %add_multiply_fusion.1), kind=kOutput, calls=%fused_computation.43 | convolution fusion | flops 6445596672 | bytes 13124608 | tf_op jit(solution)/shard_map/dot_general | solution.py:56
  117.6 0.0 reduce-scatter.2.cloned.1.call-update
  117.6 0.0 all-reduce.3.cloned.1.call-start
  117.7 0.6 copy-done.9
  118.3 0.1 copy.14
  118.4 0.2 mul.141
  118.6 0.1 copy.13
  118.7 0.2 mul.135
  118.9 0.6 dynamic-slice
  120.2 0.0 copy-start.11
  120.2 3.8 fusion.23
  124.0 27.8 %all-reduce = f32[4096]{0:T(1024)S(1)} all-reduce(f32[4096]{0:T(1024)S(1)} %fusion.23), channel_id=7, replica_groups=mesh['row'=4,'col'=8] {'col'}, use_global_device_ids=true, to_apply=%region_14.15.clone | all-reduce | flops 4096 | bytes 32768
  151.8 0.1 dynamic-slice.1
  151.9 53.3 %reduce-scatter.2.cloned.1.call-done = f32[512,512]{1,0:T(8,128)} async-done(((f32[4096,512]{1,0:T(8,128)}), f32[512,512]{1,0:T(8,128)}) %reduce-scatter.2.cloned.1.call-update) | async-done | bytes 1048592 | tf_op jit(solution)/shard_map/reduce_scatter | solution.py:61
  205.2 1.8 fusion.37
  207.0 0.0 copy-start.5
  207.0 0.0 copy-start.7
  207.0 0.0 copy-start.10
  207.0 12.3 %multiply_convert_fusion.1 = (bf16[4096,1024]{1,0:T(8,128)(2,1)S(1)}, f32[4096,1024]{1,0:T(8,128)}) fusion(f32[1024]{0:T(1024)S(1)} %copy-done.11, f32[4096]{0:T(1024)S(1)} %mul.141, bf16[512,1024]{1,0:T(8,128)(2,1)S(1)} %copy-done, f32[512,512]{1,0:T(8,128)S(1)} %get-tuple-element.308, f32[512,512]{1,0:T(8,128)S(1)} %get-tuple-element.307, f32[4096]{0:T(1024)S(1)} %mul.135), kind=kOutput, calls=%fused_computation.7 | convolution fusion | flops 4332716032 | bytes 28348416 | tf_op jit(solution)/shard_map/dot_general | solution.py:79
  219.3 6.1 %fusion.38 = (bf16[4096,512]{1,0:T(8,128)(2,1)}, f32[4096,512]{1,0:T(8,128)S(1)}) fusion(bf16[4096,1024]{1,0:T(8,128)(2,1)S(1)} %get-tuple-element.317, bf16[1024,512]{1,0:T(8,128)(2,1)S(1)} %copy-done.10), kind=kOutput, calls=%fused_computation.62 | convolution fusion | flops 4297064448 | bytes 22020096 | tf_op jit(solution)/shard_map/dot_general | solution.py:83
  225.4 4.6 %fusion.28 = f32[512,1024]{1,0:T(8,128)S(1)} fusion(bf16[4096,1024]{1,0:T(8,128)(2,1)S(1)} %get-tuple-element.317, f32[4096,512]{1,0:T(8,128)S(1)} %get-tuple-element.320, f32[512,512]{1,0:T(8,128)S(1)} %get-tuple-element.306), kind=kOutput, calls=%fused_computation.48 | convolution fusion | flops 4301258752 | bytes 19922944 | tf_op jit(solution)/shard_map/dot_general | solution.py:94
  230.0 0.0 copy-start.6
  230.0 16.4 %multiply_convert_fusion.6 = bf16[4096,1024]{1,0:T(8,128)(2,1)} fusion(f32[4096,1024]{1,0:T(8,128)} %get-tuple-element.318, f32[1024]{0:T(1024)S(1)} %copy-done.11, f32[4096]{0:T(1024)S(1)} %mul.141, bf16[1024,512]{1,0:T(8,128)(2,1)} %param.15, f32[4096,512]{1,0:T(8,128)} %copy-done.13, f32[512,512]{1,0:T(8,128)} %copy-done.8), kind=kOutput, calls=%fused_computation.6.clone.clone.2 | convolution fusion | flops 4347396096 | bytes 35672064 | tf_op jit(solution)/shard_map/dot_general | solution.py:87
  246.4 8.4 %fusion.4 = f32[512,1024]{1,0:T(8,128)S(1)} fusion(f32[4096]{0:T(1024)S(1)} %mul.141, f32[512,512]{1,0:T(8,128)} %copy-done.7, f32[512,512]{1,0:T(8,128)S(1)} %copy-done.6, f32[4096]{0:T(1024)S(1)} %mul.135, bf16[4096,1024]{1,0:T(8,128)(2,1)} %multiply_convert_fusion.6), kind=kOutput, calls=%fused_computation.18 | convolution fusion | flops 4303355904 | bytes 12615680 | tf_op jit(solution)/shard_map/dot_general | solution.py:93
  254.8 2.4 pad_maximum_fusion
  257.2 0.0 all-reduce.3.cloned.1.call-update
  257.2 140.8 %all-reduce.3.cloned.1.call-done = f32[512,2048]{1,0:T(8,128)} async-done(((f32[512,2048]{1,0:T(8,128)}), f32[512,2048]{1,0:T(8,128)}) %all-reduce.3.cloned.1.call-update) | async-done | bytes 4194320 | tf_op jit(solution)/shard_map/psum | solution.py:95
  398.0 4.1 slice_bitcast_fusion
  402.1 1.8 copy.15
  (49 shorter events, 0.6 us)
Async XLA Ops:
  7.2 199.8 %copy-start = (bf16[512,1024]{1,0:T(8,128)(2,1)S(1)}, bf16[512,1024]{1,0:T(8,128)(2,1)}, u32[]{:S(2)}) copy-start(bf16[512,1024]{1,0:T(8,128)(2,1)} %param.14) | copy-start | bytes 3145732
  7.2 198.0 %reduce-scatter.2.cloned.1.call-start = ((), (), s32[]{:S(2)}) async-start(), calls=%async_computation.1 | async-start | bytes 9437184 | tf_op jit(solution)/shard_map/reduce_scatter | solution.py:61
  7.2 5.5 %copy-start.4 = (f32[256,512]{1,0:T(8,128)S(1)}, f32[256,512]{1,0:T(8,128)}, u32[]{:S(2)}) copy-start(f32[256,512]{1,0:T(8,128)} %param.11) | copy-start | bytes 1572868
  8.5 5.8 %copy-start.3 = (f32[4096,512]{1,0:T(8,128)S(1)}, f32[4096,512]{1,0:T(8,128)}, u32[]{:S(2)}) copy-start(f32[4096,512]{1,0:T(8,128)} %param.10) | copy-start | bytes 25165828
  57.0 3.5 copy-start.2
  117.6 0.7 copy-start.9
  117.6 1.3 copy-start.12
  117.6 280.4 %all-reduce.3.cloned.1.call-start = ((), (), s32[]{:S(2)}) async-start(), calls=%async_computation.2 | async-start | bytes 8388608 | tf_op jit(solution)/shard_map/psum | solution.py:95
  120.2 86.8 %copy-start.11 = (f32[1024]{0:T(1024)S(1)}, f32[1024]{0:T(1024)}, u32[]{:S(2)}) copy-start(f32[1024]{0:T(1024)} %param.13) | copy-start | bytes 12292
  207.0 12.4 %copy-start.5 = (f32[512,512]{1,0:T(8,128)}, f32[512,512]{1,0:T(8,128)S(1)}, u32[]{:S(2)}) copy-start(f32[512,512]{1,0:T(8,128)S(1)} %get-tuple-element.307) | copy-start | bytes 3145732
  207.0 12.4 %copy-start.7 = (f32[512,512]{1,0:T(8,128)}, f32[512,512]{1,0:T(8,128)S(1)}, u32[]{:S(2)}) copy-start(f32[512,512]{1,0:T(8,128)S(1)} %get-tuple-element.308) | copy-start | bytes 3145732
  207.0 18.4 %copy-start.8 = (f32[512,512]{1,0:T(8,128)}, f32[512,512]{1,0:T(8,128)S(1)}, u32[]{:S(2)}) copy-start(f32[512,512]{1,0:T(8,128)S(1)} %get-tuple-element.306) | copy-start | bytes 3145732
  207.0 12.3 %copy-start.10 = (bf16[1024,512]{1,0:T(8,128)(2,1)S(1)}, bf16[1024,512]{1,0:T(8,128)(2,1)}, u32[]{:S(2)}) copy-start(bf16[1024,512]{1,0:T(8,128)(2,1)} %param.15) | copy-start | bytes 3145732
  225.4 4.6 %copy-start.13 = (f32[4096,512]{1,0:T(8,128)}, f32[4096,512]{1,0:T(8,128)S(1)}, u32[]{:S(2)}) copy-start(f32[4096,512]{1,0:T(8,128)S(1)} %get-tuple-element.320) | copy-start | bytes 25165828
  230.0 16.4 %copy-start.6 = (f32[512,512]{1,0:T(8,128)S(1)}, f32[512,512]{1,0:T(8,128)}, u32[]{:S(2)}) copy-start(f32[512,512]{1,0:T(8,128)} %copy-done.5) | copy-start | bytes 3145732
  398.0 5.9 %copy-start.1 = (bf16[512,1024]{1,0:T(8,128)(2,1)S(1)}, bf16[512,1024]{1,0:T(8,128)(2,1)}, u32[]{:S(2)}) copy-start(bf16[512,1024]{1,0:T(8,128)(2,1)} %param.14) | copy-start | bytes 3145732
Sparse Core Ops, SparseCore 0:
  117.8 87.3 reduce-scatter.1
  257.3 140.6 all-reduce.2
where the time goes:
time: 411 us
  waiting for transfers between devices  194 us (47%)
  blocking collectives  99.8 us (24%)
  matrix products  68.1 us (17%)
  other arithmetic  23.2 us (6%)
  between operations  15 us (4%)
  local copies, waits for them, and re-layouts  10.2 us (2%)
    psum x1, waiting for transfers between devices, on_device(): summed = lax.psum(jnp.concatenate([first, second], axis=1), ('row', 'col'))  141 us
    reduce_scatter x1, waiting for transfers between devices, on_device(): lax.psum_scatter(numer, 'col', scatter_dimension=0, tiled=True)  53.3 us
    all_gather x4, blocking collectives, combined_all(): gathered = jax.tree.map(lambda a: lax.all_gather(a, axis), part)  45.8 us
    unnamed x1, blocking collectives  27.8 us
    pmax x1, blocking collectives, on_device(): final_peak = lax.pmax(jnp.max(scores, axis=1), 'col')  26.1 us
    dot_general x1, matrix products, on_device(): lax.dot_general(delta, weight_out, (((1,), (1,)), ((), ())), preferred_el...  16.4 us
    dot_general x1, matrix products, on_device(): jnp.dot(mixed, weight_in, preferred_element_type=jnp.float32)  12.3 us
    dot_general x1, matrix products, on_device(): jnp.dot(weights, data_points, precision=HIGHEST_PREC, preferred_element_t...  11.1 us
  transfers between devices with their start and end apart: 2, of which 2 were waited for; matrix products, arithmetic and copies ran while one was open for 1% of the time, Pallas kernels for 0%

commit v1 on v0

--- a/solution.py
+++ b/solution.py
@@ -92,7 +92,9 @@
     contract = (((0,), (0,)), ((), ()))
     first = lax.dot_general(mixed, delta_pre, contract, preferred_element_type=jnp.float32)
     second = lax.dot_general(delta, hidden, contract, preferred_element_type=jnp.float32)
-    summed = lax.psum(jnp.concatenate([first, second], axis=1), ("row", "col"))
+    summed = jnp.concatenate([first, second], axis=1)
+    for name in ("col", "row"):
+        summed = lax.psum(summed, name)
     grad_in = summed[:, :hid_width]
     grad_out = summed[:, hid_width:].T
     return (predicted, grad_in, grad_out)

time: 411 us -> 472 us (1.15)
  waiting for transfers between devices: 194 us -> 255 us
    psum x1 -> x2, waiting for transfers between devices: 141 us -> 202 us  [on_device(): summed = lax.psum(summed, name)]
  transfers between devices with their start and end apart: 2 -> 3, of which waited for: 2 -> 3; matrix products, arithmetic and copies ran while one was open for 1% -> 1% of each run, Pallas kernels for 0% -> 0%
where the time goes in v1:
time: 472 us; the launch traced here: 471 us
  waiting for transfers between devices  255 us (54%)
  blocking collectives  99.8 us (21%)
  matrix products  68.1 us (14%)
  other arithmetic  23.2 us (5%)
  between operations  14.7 us (3%)
  local copies, waits for them, and re-layouts  10.2 us (2%)
    psum x2, waiting for transfers between devices, on_device(): summed = lax.psum(summed, name)  202 us
    reduce_scatter x1, waiting for transfers between devices, on_device(): lax.psum_scatter(numer, 'col', scatter_dimension=0, tiled=True)  53.3 us
    all_gather x4, blocking collectives, combined_all(): gathered = jax.tree.map(lambda a: lax.all_gather(a, axis), part)  45.8 us
    unnamed x1, blocking collectives  27.8 us
    pmax x1, blocking collectives, on_device(): final_peak = lax.pmax(jnp.max(scores, axis=1), 'col')  26.1 us
    dot_general x1, matrix products, on_device(): lax.dot_general(delta, weight_out, (((1,), (1,)), ((), ())), preferred_el...  16.4 us
    dot_general x1, matrix products, on_device(): jnp.dot(mixed, weight_in, preferred_element_type=jnp.float32)  12.3 us
    dot_general x1, matrix products, on_device(): jnp.dot(weights, data_points, precision=HIGHEST_PREC, preferred_element_t...  11.1 us
  transfers between devices with their start and end apart: 3, of which 3 were waited for; matrix products, arithmetic and copies ran while one was open for 1% of the time, Pallas kernels for 0%

profile of v1, /device:TPU:0, one launch (start us, length us, event | category | flops | bytes accessed | tf_op | source)
XLA Modules:
  0.0 471.4 jit_solution(1236239797719699842)
XLA Ops:
  7.2 0.0 copy-start
  7.2 0.0 reduce-scatter.2.cloned.1.call-start
  7.2 1.3 multiply_reduce_fusion.1
  8.5 4.2 multiply_reduce_fusion
  12.7 1.6 copy-done.3
  14.3 9.3 %fusion.20 = (f32[4096]{0:T(1024)S(1)}, f32[4096,256]{0,1:T(8,128)}) fusion(f32[4096,512]{1,0:T(8,128)S(1)} %copy-done.3, f32[256,512]{1,0:T(8,128)S(1)} %copy-done.4, f32[256]{0:T(256)S(1)} %multiply_reduce_fusion.1, f32[4096]{0:T(1024)S(1)} %multiply_reduce_fusion), kind=kOutput, calls=%fused_computation.39 | convolution fusion | flops 6449786880 | bytes 13140992 | tf_op jit(solution)/shard_map/dot_general | solution.py:38
  23.6 15.7 %all-gather = f32[32768]{0:T(1024)S(1)} all-gather(f32[4096]{0:T(1024)S(1)} %get-tuple-element.315), channel_id=2, replica_groups=mesh['row'=4,'col'=8] {'col'}, dimensions={0}, use_global_device_ids=true | all-gather | bytes 147456 | tf_op jit(solution)/shard_map/all_gather | solution.py:12
  39.3 3.0 exponential_reduce_fusion.1
  42.4 14.0 %all-gather.1 = f32[32768]{0:T(1024)S(1)} all-gather(f32[4096]{0:T(1024)S(1)} %exponential_reduce_fusion.1), channel_id=3, replica_groups=mesh['row'=4,'col'=8] {'col'}, dimensions={0}, use_global_device_ids=true | all-gather | bytes 147456 | tf_op jit(solution)/shard_map/all_gather | solution.py:12
  56.4 0.6 while.34
  57.0 2.9 fusion.21
  59.9 0.6 copy-done.2
  60.4 0.9 exponential_reduce_fusion
  61.4 8.1 %all-gather.4 = f32[4,1,256]{2,1,0:T(1,128)S(1)} all-gather(f32[1,1,256]{2,1,0:T(1,128)S(1)} %bitcast.83), channel_id=4, replica_groups=mesh['row'=4,'col'=8] {'row'}, dimensions={0}, use_global_device_ids=true | all-gather | bytes 5120 | tf_op jit(solution)/shard_map/all_gather | solution.py:12
  69.5 8.0 %all-gather.5 = f32[4,1,256]{2,1,0:T(1,128)S(1)} all-gather(f32[1,1,256]{2,1,0:T(1,128)S(1)} %bitcast.84), channel_id=5, replica_groups=mesh['row'=4,'col'=8] {'row'}, dimensions={0}, use_global_device_ids=true | all-gather | bytes 5120 | tf_op jit(solution)/shard_map/all_gather | solution.py:12
  77.5 0.1 while.35
  77.7 2.8 fusion.22
  80.4 26.1 %pmax.7 = f32[4096]{0:T(1024)S(1)} all-reduce(f32[4096]{0:T(1024)S(1)} %fusion.22), channel_id=1, replica_groups=mesh['row'=4,'col'=8] {'col'}, use_global_device_ids=true, to_apply=%region_11.12 | all-reduce | flops 4096 | bytes 32768 | tf_op jit(solution)/shard_map/pmax | solution.py:54
  106.5 11.1 %fusion.24 = f32[4096,512]{1,0:T(8,128)} fusion(f32[256,512]{1,0:T(8,128)S(1)} %copy-done.4, f32[4096,256]{0,1:T(8,128)} %get-tuple-element.316, f32[4096]{0:T(1024)S(1)} %pmax.7, f32[256]{0:T(256)S(1)} %add_multiply_fusion.1), kind=kOutput, calls=%fused_computation.43 | convolution fusion | flops 6445596672 | bytes 13124608 | tf_op jit(solution)/shard_map/dot_general | solution.py:56
  117.6 0.0 reduce-scatter.2.cloned.1.call-update
  117.6 0.0 all-reduce.4.cloned.1.call-start
  117.7 0.6 copy-done.9
  118.3 0.1 copy.14
  118.4 0.2 mul.141
  118.6 0.1 copy.13
  118.7 0.2 mul.135
  118.9 0.6 dynamic-slice
  120.2 3.8 fusion.23
  124.0 27.8 %all-reduce = f32[4096]{0:T(1024)S(1)} all-reduce(f32[4096]{0:T(1024)S(1)} %fusion.23), channel_id=7, replica_groups=mesh['row'=4,'col'=8] {'col'}, use_global_device_ids=true, to_apply=%region_14.15.clone | all-reduce | flops 4096 | bytes 32768
  151.8 0.1 dynamic-slice.1
  151.9 53.3 %reduce-scatter.2.cloned.1.call-done = f32[512,512]{1,0:T(8,128)} async-done(((f32[4096,512]{1,0:T(8,128)}), f32[512,512]{1,0:T(8,128)}) %reduce-scatter.2.cloned.1.call-update) | async-done | bytes 1048592 | tf_op jit(solution)/shard_map/reduce_scatter | solution.py:61
  205.2 1.8 fusion.37
  207.0 0.0 copy-start.5
  207.0 0.0 copy-start.7
  207.0 12.3 %multiply_convert_fusion.1 = (bf16[4096,1024]{1,0:T(8,128)(2,1)S(1)}, f32[4096,1024]{1,0:T(8,128)}) fusion(f32[1024]{0:T(1024)S(1)} %copy-done.11, f32[4096]{0:T(1024)S(1)} %mul.141, bf16[512,1024]{1,0:T(8,128)(2,1)S(1)} %copy-done, f32[512,512]{1,0:T(8,128)S(1)} %get-tuple-element.308, f32[512,512]{1,0:T(8,128)S(1)} %get-tuple-element.307, f32[4096]{0:T(1024)S(1)} %mul.135), kind=kOutput, calls=%fused_computation.7 | convolution fusion | flops 4332716032 | bytes 28348416 | tf_op jit(solution)/shard_map/dot_general | solution.py:79
  219.3 6.1 %fusion.38 = (bf16[4096,512]{1,0:T(8,128)(2,1)}, f32[4096,512]{1,0:T(8,128)S(1)}) fusion(bf16[4096,1024]{1,0:T(8,128)(2,1)S(1)} %get-tuple-element.317, bf16[1024,512]{1,0:T(8,128)(2,1)S(1)} %copy-done.10), kind=kOutput, calls=%fused_computation.62 | convolution fusion | flops 4297064448 | bytes 22020096 | tf_op jit(solution)/shard_map/dot_general | solution.py:83
  225.4 4.6 fusion.28
  230.0 0.0 copy-start.6
  230.0 16.4 %multiply_convert_fusion.6 = bf16[4096,1024]{1,0:T(8,128)(2,1)} fusion(f32[4096,1024]{1,0:T(8,128)} %get-tuple-element.318, f32[1024]{0:T(1024)S(1)} %copy-done.11, f32[4096]{0:T(1024)S(1)} %mul.141, bf16[1024,512]{1,0:T(8,128)(2,1)} %param.15, f32[4096,512]{1,0:T(8,128)} %copy-done.13, f32[512,512]{1,0:T(8,128)} %copy-done.8), kind=kOutput, calls=%fused_computation.6.clone.clone.2 | convolution fusion | flops 4347396096 | bytes 35672064 | tf_op jit(solution)/shard_map/dot_general | solution.py:87
  246.4 8.4 %fusion.4 = f32[512,1024]{1,0:T(8,128)S(1)} fusion(f32[4096]{0:T(1024)S(1)} %mul.141, f32[512,512]{1,0:T(8,128)} %copy-done.7, f32[512,512]{1,0:T(8,128)S(1)} %copy-done.6, f32[4096]{0:T(1024)S(1)} %mul.135, bf16[4096,1024]{1,0:T(8,128)(2,1)} %multiply_convert_fusion.6), kind=kOutput, calls=%fused_computation.18 | convolution fusion | flops 4303355904 | bytes 12615680 | tf_op jit(solution)/shard_map/dot_general | solution.py:93
  254.8 2.4 pad_maximum_fusion
  257.2 0.0 all-reduce.4.cloned.1.call-update
  257.2 0.0 all-reduce.6.cloned.1.call-start
  257.2 94.8 %all-reduce.4.cloned.1.call-done = f32[512,2048]{1,0:T(8,128)} async-done(((f32[512,2048]{1,0:T(8,128)}), f32[512,2048]{1,0:T(8,128)}) %all-reduce.4.cloned.1.call-update) | async-done | bytes 4194320 | tf_op jit(solution)/shard_map/psum | solution.py:97
  352.0 0.0 all-reduce.6.cloned.1.call-update
  352.0 107.0 %all-reduce.6.cloned.1.call-done = f32[512,2048]{1,0:T(8,128)} async-done(((f32[512,2048]{1,0:T(8,128)}), f32[512,2048]{1,0:T(8,128)}) %all-reduce.6.cloned.1.call-update) | async-done | bytes 4194320 | tf_op jit(solution)/shard_map/psum | solution.py:97
  459.0 4.1 slice_bitcast_fusion
  463.1 1.8 copy.15
  (52 shorter events, 0.6 us)
Async XLA Ops:
  7.2 199.8 %copy-start = (bf16[512,1024]{1,0:T(8,128)(2,1)S(1)}, bf16[512,1024]{1,0:T(8,128)(2,1)}, u32[]{:S(2)}) copy-start(bf16[512,1024]{1,0:T(8,128)(2,1)} %param.14) | copy-start | bytes 3145732
  7.2 198.0 %reduce-scatter.2.cloned.1.call-start = ((), (), s32[]{:S(2)}) async-start(), calls=%async_computation.1 | async-start | bytes 9437184 | tf_op jit(solution)/shard_map/reduce_scatter | solution.py:61
  7.2 5.5 %copy-start.4 = (f32[256,512]{1,0:T(8,128)S(1)}, f32[256,512]{1,0:T(8,128)}, u32[]{:S(2)}) copy-start(f32[256,512]{1,0:T(8,128)} %param.11) | copy-start | bytes 1572868
  8.5 5.8 %copy-start.3 = (f32[4096,512]{1,0:T(8,128)S(1)}, f32[4096,512]{1,0:T(8,128)}, u32[]{:S(2)}) copy-start(f32[4096,512]{1,0:T(8,128)} %param.10) | copy-start | bytes 25165828
  57.0 3.5 copy-start.2
  117.6 0.7 copy-start.9
  117.6 1.3 copy-start.12
  117.6 234.4 %all-reduce.4.cloned.1.call-start = ((), (), s32[]{:S(2)}) async-start(), calls=%async_computation.2 | async-start | bytes 8388608 | tf_op jit(solution)/shard_map/psum | solution.py:97
  120.2 86.8 %copy-start.11 = (f32[1024]{0:T(1024)S(1)}, f32[1024]{0:T(1024)}, u32[]{:S(2)}) copy-start(f32[1024]{0:T(1024)} %param.13) | copy-start | bytes 12292
  207.0 12.4 %copy-start.5 = (f32[512,512]{1,0:T(8,128)}, f32[512,512]{1,0:T(8,128)S(1)}, u32[]{:S(2)}) copy-start(f32[512,512]{1,0:T(8,128)S(1)} %get-tuple-element.307) | copy-start | bytes 3145732
  207.0 12.4 %copy-start.7 = (f32[512,512]{1,0:T(8,128)}, f32[512,512]{1,0:T(8,128)S(1)}, u32[]{:S(2)}) copy-start(f32[512,512]{1,0:T(8,128)S(1)} %get-tuple-element.308) | copy-start | bytes 3145732
  207.0 18.4 %copy-start.8 = (f32[512,512]{1,0:T(8,128)}, f32[512,512]{1,0:T(8,128)S(1)}, u32[]{:S(2)}) copy-start(f32[512,512]{1,0:T(8,128)S(1)} %get-tuple-element.306) | copy-start | bytes 3145732
  207.0 12.3 %copy-start.10 = (bf16[1024,512]{1,0:T(8,128)(2,1)S(1)}, bf16[1024,512]{1,0:T(8,128)(2,1)}, u32[]{:S(2)}) copy-start(bf16[1024,512]{1,0:T(8,128)(2,1)} %param.15) | copy-start | bytes 3145732
  225.4 4.6 copy-start.13
  230.0 16.4 %copy-start.6 = (f32[512,512]{1,0:T(8,128)S(1)}, f32[512,512]{1,0:T(8,128)}, u32[]{:S(2)}) copy-start(f32[512,512]{1,0:T(8,128)} %copy-done.5) | copy-start | bytes 3145732
  257.2 201.8 %all-reduce.6.cloned.1.call-start = ((), (), s32[]{:S(2)}) async-start(), calls=%async_computation.3 | async-start | bytes 8388608 | tf_op jit(solution)/shard_map/psum | solution.py:97
  459.0 5.9 %copy-start.1 = (bf16[512,1024]{1,0:T(8,128)(2,1)S(1)}, bf16[512,1024]{1,0:T(8,128)(2,1)}, u32[]{:S(2)}) copy-start(bf16[512,1024]{1,0:T(8,128)(2,1)} %param.14) | copy-start | bytes 3145732
Sparse Core Ops, SparseCore 0:
  117.8 87.3 reduce-scatter.1
  257.3 94.6 all-reduce.3
  355.3 103.6 all-reduce.5
